TPU v7x, 32 devices: a whole 2x2x4 slice. The times are simulated.
32 devices in a mesh: st: 8 (over z, y), ob: 4 (over x, core).
Axes of the slice: x: 2, y: 2, z: 4, core: 2. Of those that a mesh axis runs over, the one named last changes fastest.
Arguments:
- ensemble: bfloat16 [18432, 64], P('st'), may hold values from -3 to 3
- weights: bfloat16 [4096, 64], P('ob'), may hold values from -6 to 6
- obs_column: int32 [4096], P('ob'), may hold values from 0 to 18431
Outputs:
- forecast: float32 [64, 3, 48, 128], P('ob', None, 'st')
All inputs are finite; a program needn't handle non-finite values.
Results may differ from a plain program's by a relative error of at most 0.0061.
Values may be sent and summed in bfloat16 or wider, within the bound.
A program may use at most 128 MiB of HBM per device.

v0:
```python
import jax
import jax.numpy as jnp
from jax import lax
from jax.sharding import PartitionSpec as P

NLON = 128
STEPS = 3
MEMBERS_PER_PART = 16
time_step = 0.3


def with_halo(block, sides, width):
    for axis, dim in sides:
        count = lax.axis_size(axis)
        forward = [(i, i + 1) for i in range(count - 1)]
        backward = [(target, source) for source, target in forward]
        low = lax.ppermute(
            lax.slice_in_dim(block, block.shape[dim] - width, None, axis=dim), axis, forward
        )
        high = lax.ppermute(lax.slice_in_dim(block, 0, width, axis=dim), axis, backward)
        block = jnp.concatenate([low, block, high], axis=dim)
    return block


def tapering(state_rows, columns, radius):
    state_lat = state_rows // (3 * NLON)
    state_lon = state_rows % NLON
    obs_lat = columns // (3 * NLON)
    obs_lon = columns % NLON
    lat_gap = state_lat[:, None] - obs_lat[None, :]
    lon_gap = jnp.abs(state_lon[:, None] - obs_lon[None, :])
    lon_gap = jnp.minimum(lon_gap, NLON - lon_gap)
    squared = (lat_gap * lat_gap + lon_gap * lon_gap).astype(jnp.float32)
    falloff = jnp.maximum(jnp.float32(0.0), 1.0 - squared / jnp.float32(radius * radius))
    return falloff * falloff


def advance(padded, latitude, lat_count):
    centre = padded[:, :, 1:-1]
    northern = padded[:, :, 2:]
    southern = padded[:, :, :-2]
    eastern = jnp.roll(centre, -1, axis=3)
    western = jnp.roll(centre, 1, axis=3)
    flux_east = (1.0 + padded[:, 0]) * padded[:, 1]
    flux_north = (1.0 + padded[:, 0]) * padded[:, 2]
    mid_east = flux_east[:, 1:-1]
    divergence = (jnp.roll(mid_east, -1, axis=2) - jnp.roll(mid_east, 1, axis=2)) / 2.0
    divergence = divergence + (flux_north[:, 2:] - flux_north[:, :-2]) / 2.0
    along_lon = (eastern - western) / 2.0
    along_lat = (northern - southern) / 2.0
    eastward = centre[:, 1]
    northward = centre[:, 2]
    coriolis = 0.8 * jnp.sin(jnp.pi * ((latitude.astype(jnp.float32) + 0.5) / lat_count - 0.5))
    coriolis = coriolis[None, :, None]
    tend_east = (
        eastward * along_lon[:, 1]
        + northward * along_lat[:, 1]
        + along_lon[:, 0]
        - coriolis * northward
    )
    tend_north = (
        eastward * along_lon[:, 2]
        + northward * along_lat[:, 2]
        + along_lat[:, 0]
        + coriolis * eastward
    )
    tendency = jnp.stack([divergence, tend_east, tend_north], axis=1)
    return 0.25 * (northern + southern + eastern + western) - time_step * tendency


def local(ensemble, weights, obs_column):
    row_count = ensemble.shape[0]
    members = ensemble.shape[1]
    lat_here = row_count // (3 * NLON)
    lat_count = lat_here * lax.axis_size("st")
    predicted_rows = ensemble.astype(jnp.float32)
    ensemble_mean = jnp.mean(predicted_rows, axis=1, keepdims=True)
    member_anomalies = (predicted_rows - ensemble_mean).astype(jnp.bfloat16)
    row_start = lax.axis_index("st") * row_count
    offset = obs_column - row_start
    inside_band = (offset >= 0) & (offset < row_count)
    clipped = jnp.clip(offset, 0, row_count - 1)
    picked = jnp.take(member_anomalies, clipped, axis=0)
    partial_value = jnp.where(inside_band[:, None], picked, jnp.zeros_like(picked)).astype(
        jnp.float32
    )
    obs_anom = lax.psum(partial_value.astype(jnp.bfloat16), "st")
    state_rows = row_start + jnp.arange(row_count, dtype=jnp.int32)
    covariance = lax.dot_general(
        member_anomalies, obs_anom, (((1,), (1,)), ((), ())), preferred_element_type=jnp.float32
    )
    kalman_gain = (
        covariance * tapering(state_rows, obs_column, lat_count) / jnp.float32(members - 1)
    ).astype(jnp.bfloat16)
    state_update = jnp.dot(kalman_gain, weights, preferred_element_type=jnp.float32)
    first_member = lax.axis_index("ob") * MEMBERS_PER_PART
    local_rows = lax.dynamic_slice_in_dim(predicted_rows, first_member, MEMBERS_PER_PART, 1)
    shared = lax.psum_scatter(state_update, "ob", scatter_dimension=1, tiled=True)
    updated_members = local_rows + shared
    fields = updated_members.reshape(lat_here, 3, NLON, MEMBERS_PER_PART).transpose(3, 1, 0, 2)
    band_start = lax.axis_index("st") * lat_here
    extended = with_halo(fields, (("st", 2),), STEPS)
    first_row = band_start - STEPS
    for section in range(STEPS):
        kept = extended.shape[2] - 2
        latitude = first_row + section + 1 + jnp.arange(kept, dtype=jnp.int32)
        extended = advance(extended, latitude, lat_count)
        inside = (latitude >= 0) & (latitude < lat_count)
        extended = jnp.where(inside[None, None, :, None], extended, jnp.float32(0.0))
    fields = extended
    return fields


def solution(mesh):
    return jax.shard_map(
        local,
        mesh=mesh,
        in_specs=(P("st", None), P("ob", None), P("ob")),
        out_specs=P("ob", None, "st", None),
        check_vma=False,
    )
```

profile of v0, /device:TPU:8, one launch (start us, length us, event | category | flops | bytes accessed | tf_op | source)
XLA Modules:
  0.0 139.1 jit_solution(10574656669796040680)
XLA Ops:
  6.5 0.7 add_select_fusion.3
  7.3 0.7 compare_and_fusion.1
  8.0 1.0 convert_reduce_fusion
  9.0 1.0 subtract_convert_fusion
  10.0 0.3 copy.60
  10.4 3.2 %gather_fusion = bf16[1024,64]{1,0:T(8,128)(2,1)S(1)} fusion(bf16[2304,64]{1,0:T(8,128)(2,1)S(1)} %copy.60, s32[1024]{0:T(1024)S(1)} %get-tuple-element.44), kind=kCustom, calls=%fused_computation | custom fusion | bytes 266240 | tf_op jit(solution)/shard_map/jit(_take)/gather | solution.py:83
  13.6 1.0 select_select_fusion
  14.7 71.7 %all-reduce.2.cloned.1.call-done = bf16[1024,64]{1,0:T(8,128)(2,1)} async-done(((bf16[1024,64]{1,0:T(8,128)(2,1)}), bf16[1024,64]{1,0:T(8,128)(2,1)}) %all-reduce.2.cloned.1.call-update) | async-done | bytes 131088 | tf_op jit(solution)/shard_map/psum | solution.py:87
  86.4 8.5 %fusion.10 = f32[2304,64]{0,1:T(8,128)} fusion(bf16[1024,64]{0,1:T(8,128)(2,1)S(1)} %copy-done, bf16[2304,64]{0,1:T(8,128)(2,1)S(1)} %subtract_convert_fusion, bf16[1024,64]{1,0:T(8,128)(2,1)} %all-reduce.2.cloned.1.call-done, s32[1024]{0:T(1024)S(1)} %get-tuple-element.45, s32[2304]{0:T(1024)S(1)} %get-tuple-element.48, s32[1024]{0:T(1024)S(1)} %get-tuple-element.43, ...), kind=kOutput, calls=%fused_computation.12 | convolution fusion | flops 641728512 | bytes 1173504 | tf_op jit(solution)/shard_map/dot_general | solution.py:95
  95.0 0.9 copy-done.1
  96.1 20.7 %reduce-scatter.2.cloned.1.call-done = f32[2304,16]{0,1:T(8,128)} async-done(((f32[2304,64]{0,1:T(8,128)}), f32[2304,16]{0,1:T(8,128)}) %reduce-scatter.2.cloned.1.call-update) | async-done | bytes 147472 | tf_op jit(solution)/shard_map/reduce_scatter | solution.py:98
  116.9 0.9 dynamic-slice_add_fusion
  117.9 3.3 %collective-permute-start.1 = (f32[16,3,3,128]{3,0,2,1:T(8,128)S(1)}, f32[16,3,3,128]{3,0,2,1:T(8,128)S(1)}, u32[]{:S(2)}, u32[]{:S(2)}) collective-permute-start(f32[16,3,3,128]{3,0,2,1:T(8,128)S(1)} %get-tuple-element.30), channel_id=1, source_target_pairs={{4,0},{8,4},{12,8},{16,12},{20,16},{24,20},{28,24},{5,1},{9,5},{13... | collective-permute-start | bytes 221192 | tf_op jit(solution)/shard_map/ppermute | solution.py:20
  121.3 2.5 %collective-permute-start = (f32[16,3,3,128]{3,0,2,1:T(8,128)S(1)}, f32[16,3,3,128]{3,0,2,1:T(8,128)S(1)}, u32[]{:S(2)}, u32[]{:S(2)}) collective-permute-start(f32[16,3,3,128]{3,0,2,1:T(8,128)S(1)} %get-tuple-element.29), channel_id=1, source_target_pairs={{0,4},{4,8},{8,12},{12,16},{16,20},{20,24},{24,28},{1,5},{5,9},{9,... | collective-permute-start | bytes 221192 | tf_op jit(solution)/shard_map/ppermute | solution.py:17
  123.8 0.4 collective-permute-done.1
  124.2 4.3 %collective-permute-done = f32[16,3,3,128]{3,0,2,1:T(8,128)S(1)} collective-permute-done((f32[16,3,3,128]{3,0,2,1:T(8,128)S(1)}, f32[16,3,3,128]{3,0,2,1:T(8,128)S(1)}, u32[]{:S(2)}, u32[]{:S(2)}) %collective-permute-start) | collective-permute-done | bytes 73760 | tf_op jit(solution)/shard_map/ppermute | solution.py:17
  128.5 0.1 fusion.57
  128.6 0.1 fusion.58
  129.0 0.2 subtract_multiply_fusion.1
  129.2 0.1 fusion.23
  129.3 0.1 fusion.27
  129.4 0.2 fusion.12
  129.6 0.1 fusion.59
  129.7 0.1 fusion.60
  130.1 0.2 subtract_multiply_fusion.3
  130.3 0.1 fusion.36
  130.4 0.2 fusion.14
  130.6 0.1 fusion.61
  130.7 0.1 fusion.62
  131.0 0.2 subtract_multiply_fusion.5
  131.3 0.1 fusion.43
  131.4 0.8 fusion.16
  (34 shorter events, 1.2 us)
Async XLA Ops:
  6.5 79.9 %copy-start = (bf16[1024,64]{0,1:T(8,128)(2,1)S(1)}, bf16[1024,64]{0,1:T(8,128)(2,1)}, u32[]{:S(2)}) copy-start(bf16[1024,64]{0,1:T(8,128)(2,1)} %param.4) | copy-start | bytes 393220
  6.5 79.9 %all-reduce.2.cloned.1.call-start = ((), (), s32[]{:S(2)}) async-start(), calls=%async_computation.1 | async-start | bytes 524288 | tf_op jit(solution)/shard_map/psum | solution.py:87
  14.6 102.2 %reduce-scatter.2.cloned.1.call-start = ((), (), s32[]{:S(2)}) async-start(), calls=%async_computation.2 | async-start | bytes 737280 | tf_op jit(solution)/shard_map/reduce_scatter | solution.py:98
  94.9 1.0 copy-start.1
  117.9 6.2 %collective-permute-start.1 = (f32[16,3,3,128]{3,0,2,1:T(8,128)S(1)}, f32[16,3,3,128]{3,0,2,1:T(8,128)S(1)}, u32[]{:S(2)}, u32[]{:S(2)}) collective-permute-start(f32[16,3,3,128]{3,0,2,1:T(8,128)S(1)} %get-tuple-element.30), channel_id=1, source_target_pairs={{4,0},{8,4},{12,8},{16,12},{20,16},{24,20},{28,24},{5,1},{9,5},{13... | collective-permute-start | bytes 221192 | tf_op jit(solution)/shard_map/ppermute | solution.py:20
  121.3 7.1 %collective-permute-start = (f32[16,3,3,128]{3,0,2,1:T(8,128)S(1)}, f32[16,3,3,128]{3,0,2,1:T(8,128)S(1)}, u32[]{:S(2)}, u32[]{:S(2)}) collective-permute-start(f32[16,3,3,128]{3,0,2,1:T(8,128)S(1)} %get-tuple-element.29), channel_id=1, source_target_pairs={{0,4},{4,8},{8,12},{12,16},{16,20},{20,24},{24,28},{1,5},{5,9},{9,... | collective-permute-start | bytes 221192 | tf_op jit(solution)/shard_map/ppermute | solution.py:17
Sparse Core Ops, SparseCore 0:
  14.8 71.6 all-reduce.1
  95.1 21.7 reduce-scatter.1
where the time goes:
time: 139 us
  waiting for transfers between devices  97.1 us (70%)
  between operations  13.7 us (10%)
  matrix products  8.5 us (6%)
  other arithmetic  8.14 us (6%)
  starting transfers between devices  5.89 us (4%)
  local copies, waits for them, and re-layouts  5.74 us (4%)
    psum x1, waiting for transfers between devices, local(): obs_anom = lax.psum(partial_value.astype(jnp.bfloat16), 'st')  71.7 us
    reduce_scatter x1, waiting for transfers between devices, local(): lax.psum_scatter(state_update, 'ob', scatter_dimension=1, tiled=True)  20.7 us
    dot_general x1, matrix products, local(): jnp.dot(kalman_gain, weights, preferred_element_type=jnp.float32)  8.5 us
    ppermute x1, waiting for transfers between devices, with_halo(): lax.ppermute(lax.slice_in_dim(block, block.shape[dim] - width, None, axis...  4.25 us
    ppermute x1, starting transfers between devices, with_halo(): lax.ppermute(lax.slice_in_dim(block, 0, width, axis=dim), axis, backward)  3.35 us
    gather x1, local copies, waits for them, and re-layouts, local(): picked = jnp.take(member_anomalies, clipped, axis=0)  3.21 us
  transfers between devices with their start and end apart: 4, of which 4 were waited for; matrix products, arithmetic and copies ran while one was open for 0% of the time, Pallas kernels for 0%

commit v1 on v0

--- a/solution.py
+++ b/solution.py
@@ -84,7 +84,12 @@
     partial_value = jnp.where(inside_band[:, None], picked, jnp.zeros_like(picked)).astype(
         jnp.float32
     )
-    obs_anom = lax.psum(partial_value.astype(jnp.bfloat16), "st")
+
+    def _meet_group(in_array):
+        new = lax.all_gather(in_array, "st").sum(axis=0)
+        return new
+
+    obs_anom = _meet_group(partial_value.astype(jnp.bfloat16))
     state_rows = row_start + jnp.arange(row_count, dtype=jnp.int32)
     covariance = lax.dot_general(
         member_anomalies, obs_anom, (((1,), (1,)), ((), ())), preferred_element_type=jnp.float32

time: 139 us -> 108 us (0.78)
  waiting for transfers between devices: 97.1 us -> 66.8 us
    psum x1 -> x0, waiting for transfers between devices: 71.7 us -> none  [local(): obs_anom = lax.psum(partial_value.astype(jnp.bfloat16), 'st')]
    all_gather x0 -> x1, waiting for transfers between devices: none -> 40.4 us  [_meet_group(): new = lax.all_gather(in_array, 'st').sum(axis=0)]
    reduce_sum x0 -> x1, other arithmetic: none -> 1.41 us  [_meet_group(): new = lax.all_gather(in_array, 'st').sum(axis=0)]
where the time goes in v1:
time: 108 us
  waiting for transfers between devices  66.8 us (62%)
  between operations  13.7 us (13%)
  other arithmetic  8.85 us (8%)
  matrix products  7.27 us (7%)
  starting transfers between devices  5.89 us (5%)
  local copies, waits for them, and re-layouts  5.6 us (5%)
    all_gather x1, waiting for transfers between devices, _meet_group(): new = lax.all_gather(in_array, 'st').sum(axis=0)  40.4 us
    reduce_scatter x1, waiting for transfers between devices, local(): lax.psum_scatter(state_update, 'ob', scatter_dimension=1, tiled=True)  21.8 us
    dot_general x1, matrix products, local(): jnp.dot(kalman_gain, weights, preferred_element_type=jnp.float32)  7.27 us
    ppermute x1, waiting for transfers between devices, with_halo(): lax.ppermute(lax.slice_in_dim(block, block.shape[dim] - width, None, axis...  4.26 us
    ppermute x1, starting transfers between devices, with_halo(): lax.ppermute(lax.slice_in_dim(block, 0, width, axis=dim), axis, backward)  3.35 us
    gather x1, local copies, waits for them, and re-layouts, local(): picked = jnp.take(member_anomalies, clipped, axis=0)  3.21 us
    ppermute x1, starting transfers between devices, with_halo(): lax.ppermute(lax.slice_in_dim(block, block.shape[dim] - width, None, axis...  2.49 us
  transfers between devices with their start and end apart: 4, of which 4 were waited for; matrix products, arithmetic and copies ran while one was open for 0% of the time, Pallas kernels for 0%

profile of v1, /device:TPU:8, one launch (start us, length us, event | category | flops | bytes accessed | tf_op | source)
XLA Modules:
  0.0 108.2 jit_solution(7016573877475819160)
XLA Ops:
  6.5 0.7 add_select_fusion.3
  7.3 0.7 compare_and_fusion.1
  8.0 1.0 convert_reduce_fusion
  9.0 1.0 subtract_convert_fusion
  10.0 0.3 copy.88
  10.4 3.2 %gather_fusion = bf16[1024,64]{1,0:T(8,128)(2,1)S(1)} fusion(bf16[2304,64]{1,0:T(8,128)(2,1)S(1)} %copy.88, s32[1024]{0:T(1024)S(1)} %get-tuple-element.44), kind=kCustom, calls=%fused_computation | custom fusion | bytes 266240 | tf_op jit(solution)/shard_map/jit(_take)/gather | solution.py:83
  13.6 0.3 fusion.11
  13.9 0.8 copy.89
  14.8 40.4 %all-gather.2.cloned.1.call-done = bf16[8,1024,64]{1,2,0:T(8,128)(2,1)} async-done(((bf16[1,1024,64]{1,2,0:T(8,128)(2,1)}), bf16[8,1024,64]{1,2,0:T(8,128)(2,1)}) %all-gather.2.cloned.1.call-update) | async-done | bytes 1048592 | tf_op jit(solution)/shard_map/all_gather | solution.py:89
  55.2 1.4 %reduce_sum.22 = bf16[1024,64]{0,1:T(8,128)(2,1)S(1)} reduce(bf16[8,1024,64]{1,2,0:T(8,128)(2,1)} %all-gather.2.cloned.1.call-done, bf16[]{:T(256)} %constant.85.clone.1), dimensions={0}, to_apply=%region_1.2 | reduce | flops 458752 | bytes 1179650 | tf_op jit(solution)/shard_map/reduce_sum | solution.py:89
  56.6 7.3 %fusion.10 = f32[2304,64]{0,1:T(8,128)} fusion(bf16[1024,64]{0,1:T(8,128)(2,1)S(1)} %copy-done, bf16[2304,64]{0,1:T(8,128)(2,1)S(1)} %subtract_convert_fusion, bf16[1024,64]{0,1:T(8,128)(2,1)S(1)} %reduce_sum.22, s32[1024]{0:T(1024)S(1)} %get-tuple-element.45, s32[2304]{0:T(1024)S(1)} %get-tuple-element.48, s32[1024]{0:T(1024)S(1)} %get-tuple-element.43, ...), kind=kOutput, calls=%fused_computation.12 | convolution fusion | flops 641728512 | bytes 1173504 | tf_op jit(solution)/shard_map/dot_general | solution.py:100
  64.1 21.8 %reduce-scatter.2.cloned.1.call-done = f32[2304,16]{0,1:T(8,128)} async-done(((f32[2304,64]{0,1:T(8,128)}), f32[2304,16]{0,1:T(8,128)}) %reduce-scatter.2.cloned.1.call-update) | async-done | bytes 147472 | tf_op jit(solution)/shard_map/reduce_scatter | solution.py:103
  86.0 0.9 dynamic-slice_add_fusion
  87.0 3.4 %collective-permute-start.1 = (f32[16,3,3,128]{3,0,2,1:T(8,128)S(1)}, f32[16,3,3,128]{3,0,2,1:T(8,128)S(1)}, u32[]{:S(2)}, u32[]{:S(2)}) collective-permute-start(f32[16,3,3,128]{3,0,2,1:T(8,128)S(1)} %get-tuple-element.30), channel_id=1, source_target_pairs={{4,0},{8,4},{12,8},{16,12},{20,16},{24,20},{28,24},{5,1},{9,5},{13... | collective-permute-start | bytes 221192 | tf_op jit(solution)/shard_map/ppermute | solution.py:20
  90.4 2.5 %collective-permute-start = (f32[16,3,3,128]{3,0,2,1:T(8,128)S(1)}, f32[16,3,3,128]{3,0,2,1:T(8,128)S(1)}, u32[]{:S(2)}, u32[]{:S(2)}) collective-permute-start(f32[16,3,3,128]{3,0,2,1:T(8,128)S(1)} %get-tuple-element.29), channel_id=1, source_target_pairs={{0,4},{4,8},{8,12},{12,16},{16,20},{20,24},{24,28},{1,5},{5,9},{9,... | collective-permute-start | bytes 221192 | tf_op jit(solution)/shard_map/ppermute | solution.py:17
  92.9 0.4 collective-permute-done.1
  93.3 4.3 %collective-permute-done = f32[16,3,3,128]{3,0,2,1:T(8,128)S(1)} collective-permute-done((f32[16,3,3,128]{3,0,2,1:T(8,128)S(1)}, f32[16,3,3,128]{3,0,2,1:T(8,128)S(1)}, u32[]{:S(2)}, u32[]{:S(2)}) %collective-permute-start) | collective-permute-done | bytes 73760 | tf_op jit(solution)/shard_map/ppermute | solution.py:17
  97.6 0.1 fusion.58
  97.7 0.1 fusion.59
  98.1 0.2 subtract_multiply_fusion.1
  98.4 0.1 fusion.28
  98.5 0.2 fusion.13
  98.7 0.1 fusion.60
  98.8 0.1 fusion.61
  99.2 0.2 subtract_multiply_fusion.3
  99.4 0.1 fusion.37
  99.5 0.2 fusion.15
  99.7 0.1 fusion.62
  99.8 0.1 fusion.63
  100.2 0.2 subtract_multiply_fusion.5
  100.4 0.1 fusion.44
  100.5 0.8 fusion.17
  (36 shorter events, 1.3 us)
Async XLA Ops:
  6.5 50.0 %copy-start = (bf16[1024,64]{0,1:T(8,128)(2,1)S(1)}, bf16[1024,64]{0,1:T(8,128)(2,1)}, u32[]{:S(2)}) copy-start(bf16[1024,64]{0,1:T(8,128)(2,1)} %param.4) | copy-start | bytes 393220
  6.5 48.6 %all-gather.2.cloned.1.call-start = ((), (), s32[]{:S(2)}) async-start(), calls=%async_computation.1 | async-start | bytes 1179648 | tf_op jit(solution)/shard_map/all_gather | solution.py:89
  14.7 71.2 %reduce-scatter.2.cloned.1.call-start = ((), (), s32[]{:S(2)}) async-start(), calls=%async_computation.2 | async-start | bytes 737280 | tf_op jit(solution)/shard_map/reduce_scatter | solution.py:103
  56.6 7.3 %copy-start.1 = (bf16[2304,64]{0,1:T(8,128)(2,1)S(1)}, bf16[2304,64]{0,1:T(8,128)(2,1)}, u32[]{:S(2)}) copy-start(bf16[2304,64]{0,1:T(8,128)(2,1)} %param.3) | copy-start | bytes 884740
  87.0 6.2 %collective-permute-start.1 = (f32[16,3,3,128]{3,0,2,1:T(8,128)S(1)}, f32[16,3,3,128]{3,0,2,1:T(8,128)S(1)}, u32[]{:S(2)}, u32[]{:S(2)}) collective-permute-start(f32[16,3,3,128]{3,0,2,1:T(8,128)S(1)} %get-tuple-element.30), channel_id=1, source_target_pairs={{4,0},{8,4},{12,8},{16,12},{20,16},{24,20},{28,24},{5,1},{9,5},{13... | collective-permute-start | bytes 221192 | tf_op jit(solution)/shard_map/ppermute | solution.py:20
  90.4 7.1 %collective-permute-start = (f32[16,3,3,128]{3,0,2,1:T(8,128)S(1)}, f32[16,3,3,128]{3,0,2,1:T(8,128)S(1)}, u32[]{:S(2)}, u32[]{:S(2)}) collective-permute-start(f32[16,3,3,128]{3,0,2,1:T(8,128)S(1)} %get-tuple-element.29), channel_id=1, source_target_pairs={{0,4},{4,8},{8,12},{12,16},{16,20},{20,24},{24,28},{1,5},{5,9},{9,... | collective-permute-start | bytes 221192 | tf_op jit(solution)/shard_map/ppermute | solution.py:17
Sparse Core Ops, SparseCore 0:
  14.8 40.2 all-gather.1
  64.0 21.9 reduce-scatter.1
